TPU v7x, 768 devices: a whole 4x8x12 slice. The times are simulated.
768 devices in a mesh: dp: 32 (over z_hi, y), tensor: 24 (over x, z_lo, core).
Axes of the slice: x: 4, y: 8, z: 12 (z_hi: 4, z_lo: 3; z = z_hi * 3 + z_lo), core: 2. Of those that a mesh axis runs over, the one named last changes fastest.
Arguments:
- activations: bfloat16 [30720, 29568], P('dp', 'tensor'), may hold values from -6 to 6
- out_grad: bfloat16 [30720, 8192], P(('dp', 'tensor')), may hold values from -6 to 6
- projector: bfloat16 [8192, 512], replicated, may hold values from -0.0625 to 0.0625
- moment_one: float32 [512, 29568], P('dp', 'tensor'), may hold values from -3.01 to 3.01
- moment_two: float32 [512, 29568], P('dp', 'tensor'), may hold values from 0.001 to 1.001
Outputs:
- weight_step: bfloat16 [29568, 8192], P('tensor', 'dp')
- new_moment_one: float32 [512, 29568], P('dp', 'tensor')
- new_moment_two: float32 [512, 29568], P('dp', 'tensor')
All inputs are finite; a program needn't handle non-finite values.
Results may differ from a plain program's by a relative error of at most 0.0056.
Values may be sent and summed in bfloat16 or wider, within the bound.
A program may use at most 32 MiB of HBM per device.

v0:
```python
import math

import jax
import jax.numpy as jnp
from jax import lax
from jax.sharding import PartitionSpec as P

beta_one = 0.9
beta_two = 0.999
epsilon = 1e-08
bias_one = 1.0 - math.exp(1000.0 * math.log(0.9))
bias_two = 1.0 - math.exp(1000.0 * math.log(0.999))


def per_device(activations, out_grad, projector, moment_one, moment_two):
    local_rows = jnp.dot(out_grad, projector, preferred_element_type=jnp.float32).astype(
        jnp.bfloat16
    )
    projected = lax.all_gather(local_rows, "tensor", axis=0, tiled=True)
    summed = lax.psum_scatter(
        lax.dot_general(
            projected, activations, (((0,), (0,)), ((), ())), preferred_element_type=jnp.float32
        ),
        "dp",
        scatter_dimension=0,
        tiled=True,
    )
    tokens_all = out_grad.shape[0] * lax.axis_size("tensor") * lax.axis_size("dp")
    gradient = summed * (1.0 / math.sqrt(tokens_all))
    new_one = beta_one * moment_one + (1.0 - beta_one) * gradient
    new_two = beta_two * moment_two + (1.0 - beta_two) * gradient * gradient
    update = (new_one / bias_one / (jnp.sqrt(new_two / bias_two) + epsilon)).astype(jnp.bfloat16)
    column_count = projector.shape[0] // lax.axis_size("dp")
    rows_mine = lax.dynamic_slice_in_dim(
        projector, lax.axis_index("dp") * column_count, column_count, 0
    )
    gathered_update = lax.all_gather(update, "dp", axis=0, tiled=True)
    weight_step = lax.dot_general(
        gathered_update, rows_mine, (((0,), (1,)), ((), ())), preferred_element_type=jnp.float32
    )
    return (weight_step.astype(jnp.bfloat16), new_one, new_two)


def solution(mesh):
    placed = (
        P("dp", "tensor"),
        P(("dp", "tensor"), None),
        P(),
        P("dp", "tensor"),
        P("dp", "tensor"),
    )
    return jax.shard_map(
        per_device,
        mesh=mesh,
        in_specs=placed,
        out_specs=(P("tensor", "dp"), P("dp", "tensor"), P("dp", "tensor")),
        check_vma=False,
    )
```

profile of v0, /device:TPU:2, one launch (start us, length us, event | category | flops | bytes accessed | tf_op | source)
XLA Modules:
  0.0 406.6 jit_solution(7342475118150610522)
XLA Ops:
  7.2 0.0 copy-start
  7.2 0.0 reduce-scatter.2.cloned.1.call-start
  7.2 5.3 %convolution_convert_fusion.1 = bf16[40,512]{1,0:T(8,128)(2,1)S(1)} fusion(bf16[40,8192]{1,0:T(8,128)(2,1)} %param.6, bf16[8192,512]{1,0:T(8,128)(2,1)} %param.7), kind=kOutput, calls=%fused_computation.1 | convolution fusion | flops 335564800 | bytes 9084928 | tf_op jit(solution)/shard_map/dot_general | solution.py:16
  12.5 36.4 %all_gather.6 = bf16[960,512]{1,0:T(8,128)(2,1)S(1)} all-gather(bf16[40,512]{1,0:T(8,128)(2,1)S(1)} %convolution_convert_fusion.1), channel_id=1, replica_groups=mesh['dp'=32,'tensor'=24] {'tensor'}, dimensions={0}, use_global_device_ids=true | all-gather | bytes 1024000 | tf_op jit(solution)/shard_map/all_gather | solution.py:19
  48.9 0.0 copy-done
  48.9 3.1 fusion.2
  51.9 0.0 copy-start.1
  51.9 0.0 copy-start.2
  51.9 0.0 reduce-scatter.2.cloned.1.call-update
  52.0 0.0 all-gather.2.cloned.1.call-start
  52.0 249.0 %reduce-scatter.2.cloned.1.call-done = f32[16,1232]{1,0:T(8,128)} async-done(((f32[512,1232]{1,0:T(8,128)}), f32[16,1232]{1,0:T(8,128)}) %reduce-scatter.2.cloned.1.call-update) | async-done | bytes 78864 | tf_op jit(solution)/shard_map/reduce_scatter | solution.py:20
  301.0 0.0 copy-done.1
  301.0 0.0 copy-done.2
  301.0 1.6 divide_convert_fusion
  302.6 0.0 all-gather.2.cloned.1.call-update
  302.6 94.4 %all-gather.2.cloned.1.call-done = bf16[512,1232]{1,0:T(8,128)(2,1)} async-done(((bf16[16,1232]{1,0:T(8,128)(2,1)}), bf16[512,1232]{1,0:T(8,128)(2,1)}) %all-gather.2.cloned.1.call-update) | async-done | bytes 1261584 | tf_op jit(solution)/shard_map/all_gather | solution.py:37
  397.0 2.7 convolution_convert_fusion
Async XLA Ops:
  7.2 41.7 %copy-start = (bf16[960,1232]{1,0:T(8,128)(2,1)S(1)}, bf16[960,1232]{1,0:T(8,128)(2,1)}, u32[]{:S(2)}) copy-start(bf16[960,1232]{1,0:T(8,128)(2,1)} %param.5) | copy-start | bytes 7096324
  7.2 293.8 %reduce-scatter.2.cloned.1.call-start = ((), (), s32[]{:S(2)}) async-start(), calls=%async_computation.1 | async-start | bytes 2703360 | tf_op jit(solution)/shard_map/reduce_scatter | solution.py:20
  51.9 249.0 %copy-start.1 = (f32[16,1232]{1,0:T(8,128)S(1)}, f32[16,1232]{1,0:T(8,128)}, u32[]{:S(2)}) copy-start(f32[16,1232]{1,0:T(8,128)} %param.9) | copy-start | bytes 236548
  51.9 249.0 %copy-start.2 = (f32[16,1232]{1,0:T(8,128)S(1)}, f32[16,1232]{1,0:T(8,128)}, u32[]{:S(2)}) copy-start(f32[16,1232]{1,0:T(8,128)} %param.8) | copy-start | bytes 236548
  52.0 345.1 %all-gather.2.cloned.1.call-start = ((), (), s32[]{:S(2)}) async-start(), calls=%async_computation.2 | async-start | bytes 1351680 | tf_op jit(solution)/shard_map/all_gather | solution.py:37
Sparse Core Ops, SparseCore 0:
  52.1 248.8 reduce-scatter.1
  305.3 91.6 all-gather.1
where the time goes:
time: 407 us
  waiting for transfers between devices  343 us (84%)
  blocking collectives  36.4 us (9%)
  between operations  14.1 us (3%)
  matrix products  11.1 us (3%)
    reduce_scatter x1, waiting for transfers between devices, per_device(): lax.psum_scatter(lax.dot_general(projected, activations, (((0,), (0,)), (...  249 us
    all_gather x1, waiting for transfers between devices, per_device(): gathered_update = lax.all_gather(update, 'dp', axis=0, tiled=True)  94.4 us
    all_gather x1, blocking collectives, per_device(): projected = lax.all_gather(local_rows, 'tensor', axis=0, tiled=True)  36.4 us
  transfers between devices with their start and end apart: 2, of which 2 were waited for; matrix products, arithmetic and copies ran while one was open for 0% of the time, Pallas kernels for 0%

commit v1 on v0

v1 whole, which is shorter than its diff:
```python
import functools
import math

import jax
import jax.numpy as jnp
from jax import lax
from jax.experimental import pallas as pl
from jax.experimental.pallas import tpu as pltpu
from jax.sharding import PartitionSpec as P

beta_one = 0.9
beta_two = 0.999
epsilon = 1e-08
bias_one = 1.0 - math.exp(1000.0 * math.log(0.9))
bias_two = 1.0 - math.exp(1000.0 * math.log(0.999))

NY, NZ = 8, 4
NX, NL, NC = 4, 3, 2
NT = NX * NL * NC
ND = NY * NZ
ROWS = 40
RANK = 512
OWN = RANK // ND
TOK = ROWS * NT
COLS = 1232
WIDE = 1280
DM = 8192
OUT = DM // ND
KC = 1024
SCALE = 1.0 / math.sqrt(ROWS * NT * ND)

RS_ORDER = (2, 1, 3, 0)
AG_ORDER = (0, 1, 3, 2)
RIGHT_HOPS = {2: 4, 1: 3, 3: 4, 0: 3}


def hops(o, way):
    return RIGHT_HOPS[o] if way == 0 else 7 - RIGHT_HOPS[o]


def kernel(
    act_hbm, og_hbm, proj_hbm, m1_hbm, m2_hbm,
    w_hbm, n1_hbm, n2_hbm,
    og, proj, act, pslice, m1, m2, n1, n2, wout,
    blocks, tokens, grad, sums_out, sums_in, z_out, z_in, upd,
    local_sem, out_sem, a_send, a_recv, rs_send, rs_recv, zs_send, zs_recv, ag_send, ag_recv,
):
    dp = lax.axis_index("dp")
    t = lax.axis_index("tensor")
    y, z = lax.rem(dp, NY), lax.div(dp, NY)
    core = lax.rem(t, NC)
    zl = lax.rem(lax.div(t, NC), NL)
    x = lax.div(t, NC * NL)

    def tensor_at(dx, dl, dc):
        xx = lax.rem(x + dx + NX, NX)
        ll = lax.rem(zl + dl, NL)
        cc = lax.rem(core + dc, NC)
        return (xx * NL + ll) * NC + cc

    def y_at(d):
        return lax.rem(y + d + NY, NY)

    def z_at(o):
        return lax.rem(z + o, NZ)

    def dev(dp_id=None, t_id=None):
        return {"dp": dp if dp_id is None else dp_id, "tensor": t if t_id is None else t_id}

    loads = [pltpu.make_async_copy(og_hbm, og, local_sem.at[0])]
    nk = DM // KC
    for k in range(nk):
        part = pl.ds(k * KC, KC)
        loads.append(pltpu.make_async_copy(proj_hbm.at[part], proj.at[part], local_sem.at[1 + k]))
    mine = pl.ds(pl.multiple_of(dp * OUT, OUT), OUT)
    late = [
        pltpu.make_async_copy(act_hbm, act, local_sem.at[nk + 1]),
        pltpu.make_async_copy(m1_hbm, m1, local_sem.at[nk + 2]),
        pltpu.make_async_copy(m2_hbm, m2, local_sem.at[nk + 3]),
        pltpu.make_async_copy(proj_hbm.at[mine], pslice, local_sem.at[nk + 4]),
    ]
    for copy in loads + late:
        copy.start()

    barrier = pltpu.get_barrier_semaphore()
    peers = [
        dev(t_id=tensor_at(0, 0, 1)),
        dev(t_id=tensor_at(1, 0, 0)), dev(t_id=tensor_at(-1, 0, 0)),
        dev(t_id=tensor_at(0, 1, 0)), dev(t_id=tensor_at(0, 2, 0)),
        dev(dp_id=z * NY + y_at(1)), dev(dp_id=z * NY + y_at(-1)),
    ] + [dev(dp_id=z_at(o) * NY + y) for o in (1, 2, 3)]
    for peer in peers:
        pl.semaphore_signal(barrier, inc=1, device_id=peer, device_id_type=pl.DeviceIdType.MESH)

    loads[0].wait()
    acc = jnp.zeros((ROWS, RANK), jnp.float32)
    for k in range(nk):
        loads[1 + k].wait()
        acc = acc + jnp.dot(
            og[:, k * KC:(k + 1) * KC], proj[k * KC:(k + 1) * KC, :],
            preferred_element_type=jnp.float32,
        )
    blocks[t] = acc.astype(jnp.bfloat16)
    grad[:, :, WIDE - 128:] = jnp.zeros((ND, OWN, 128), jnp.float32)
    pl.semaphore_wait(barrier, len(peers))

    sent = []

    def remote(src, dst, ssem, rsem, peer):
        return pltpu.make_async_remote_copy(
            src_ref=src, dst_ref=dst, send_sem=ssem, recv_sem=rsem,
            device_id=peer, device_id_type=pl.DeviceIdType.MESH,
        )

    def send(src, dst, ssem, rsem, peer):
        copy = remote(src, dst, ssem, rsem, peer)
        copy.start()
        sent.append(copy)

    count_a = [0]
    other = dev(t_id=tensor_at(0, 0, 1))

    def send_a(slot, peer):
        n = count_a[0]
        count_a[0] += 1
        send(blocks.at[slot], blocks.at[slot], a_send.at[n], a_recv.at[slot], peer)

    def wait_a(slot):
        remote(blocks.at[slot], blocks.at[slot], a_send.at[0], a_recv.at[slot], other).wait_recv()

    east, west = dev(t_id=tensor_at(1, 0, 0)), dev(t_id=tensor_at(-1, 0, 0))
    send_a(t, east)
    send_a(t, west)
    for dl in (1, 2):
        send_a(t, dev(t_id=tensor_at(0, dl, 0)))
    send_a(t, other)
    for dl in (1, 2):
        slot = tensor_at(0, dl, 0)
        wait_a(slot)
        send_a(slot, east)
        send_a(slot, west)
        send_a(slot, other)
    for dl in range(NL):
        way = 1 - 2 * lax.rem(core + dl, 2)
        near, far = tensor_at(-way, dl, 0), tensor_at(way, dl, 0)
        wait_a(near)
        send_a(near, dev(t_id=tensor_at(way, 0, 0)))
        send_a(near, other)
        wait_a(far)
        send_a(far, other)
    for dl in range(NL):
        slot = tensor_at(2, dl, 0)
        wait_a(slot)
        send_a(slot, other)
    for dx in (0, 1, -1, 2):
        for dl in range(NL):
            wait_a(tensor_at(dx, dl, 1))
    for pair in range(NT // 2):
        both = jnp.concatenate(
            [blocks[2 * pair].astype(jnp.float32), blocks[2 * pair + 1].astype(jnp.float32)], axis=0
        )
        tokens[pair * 2 * ROWS:(pair + 1) * 2 * ROWS, :] = both.astype(jnp.bfloat16)
    late[0].wait()

    ring = (dev(dp_id=z * NY + y_at(1)), dev(dp_id=z * NY + y_at(-1)))
    index = {}
    for o in RS_ORDER:
        for way in (0, 1):
            for s in range(hops(o, way)):
                index[o, way, s] = len(index)

    def push(o, way, s):
        n = index[o, way, s]
        sign = 1 if way == 0 else -1
        row = z_at(o) * NY + y_at(sign * (hops(o, way) - s))
        value = grad[row]
        if s > 0:
            value = value + sums_in[index[o, way, s - 1]].astype(jnp.float32)
        sums_out[n] = value.astype(jnp.bfloat16)
        send(sums_out.at[n], sums_in.at[n], rs_send.at[n], rs_recv.at[n], ring[way])

    def wait_rs(o, way, s):
        n = index[o, way, s]
        remote(sums_out.at[n], sums_in.at[n], rs_send.at[n], rs_recv.at[n], ring[1 - way]).wait_recv()

    for o in RS_ORDER:
        first = pl.multiple_of(z_at(o) * 128, 128)
        tile = lax.dot_general(
            tokens[:, pl.ds(first, 128)], act[...], (((0,), (0,)), ((), ())),
            preferred_element_type=jnp.float32,
        )
        grad[pl.ds(z_at(o) * NY, NY), :, :COLS] = tile.reshape(NY, OWN, COLS)
        for way in (0, 1):
            push(o, way, 0)

    events = []
    for place, o in enumerate(RS_ORDER):
        for way in (0, 1):
            for s in range(hops(o, way)):
                events.append((place * 1.7 + s * 2.5, place, s, way, o))
    left = {o: 2 for o in RS_ORDER}
    total = None
    for _, _, s, way, o in sorted(events):
        wait_rs(o, way, s)
        if s + 1 < hops(o, way):
            push(o, way, s + 1)
            continue
        left[o] -= 1
        if left[o]:
            continue
        value = grad[z_at(o) * NY + y]
        for w in (0, 1):
            value = value + sums_in[index[o, w, hops(o, w) - 1]].astype(jnp.float32)
        if o == 0:
            total = value
        else:
            z_out[o - 1] = value.astype(jnp.bfloat16)
            send(
                z_out.at[o - 1], z_in.at[o - 1], zs_send.at[o - 1], zs_recv.at[o - 1],
                dev(dp_id=z_at(o) * NY + y),
            )

    for o in (1, 3, 2):
        remote(z_out.at[o - 1], z_in.at[o - 1], zs_send.at[o - 1], zs_recv.at[o - 1], ring[0]).wait_recv()
        total = total + z_in[o - 1].astype(jnp.float32)

    for copy in late[1:]:
        copy.wait()
    gradient = total[:, :COLS] * SCALE
    new_one = beta_one * m1[...] + (1.0 - beta_one) * gradient
    new_two = beta_two * m2[...] + (1.0 - beta_two) * gradient * gradient
    update = new_one / bias_one / (jnp.sqrt(new_two / bias_two) + epsilon)
    own = z * NY + y
    upd[own, :, WIDE - 128:] = jnp.zeros((OWN, 128), jnp.bfloat16)
    upd[own, :, :COLS] = update.astype(jnp.bfloat16)
    n1[...] = new_one
    n2[...] = new_two

    count_g = [0]

    def send_g(slot, peer):
        n = count_g[0]
        count_g[0] += 1
        send(upd.at[slot], upd.at[slot], ag_send.at[n], ag_recv.at[slot], peer)

    def wait_g(slot):
        remote(upd.at[slot], upd.at[slot], ag_send.at[0], ag_recv.at[slot], other).wait_recv()

    send_g(own, ring[0])
    send_g(own, ring[1])
    for o in (2, 1, 3):
        send_g(own, dev(dp_id=z_at(o) * NY + y))
    outs = [
        pltpu.make_async_copy(n1, n1_hbm, out_sem.at[0]),
        pltpu.make_async_copy(n2, n2_hbm, out_sem.at[1]),
    ]
    for copy in outs:
        copy.start()

    arrives = {0: 0.0, 1: 3.6, 3: 3.8, 2: 5.8}
    events = []
    for o in AG_ORDER:
        if o:
            events.append((arrives[o], 0, o, 0, -1))
        for way in (0, 1):
            for s in range(hops(o, way)):
                events.append((arrives[o] + 2.3 * (s + 1), 1, o, way, s))
    for _, _, o, way, s in sorted(events):
        base = z_at(o) * NY
        if s < 0:
            wait_g(base + y)
            send_g(base + y, ring[0])
            send_g(base + y, ring[1])
            continue
        slot = base + y_at(-(s + 1) if way == 0 else s + 1)
        wait_g(slot)
        if s + 1 < hops(o, way):
            send_g(slot, ring[way])

    for m in range(0, COLS, 256):
        width = min(256, WIDE - m)
        part = upd[:, :, m:m + width].reshape(RANK, width)
        tile = lax.dot_general(
            part, pslice[...], (((0,), (1,)), ((), ())), preferred_element_type=jnp.float32
        )
        rows = min(width, COLS - m)
        wout[m:m + rows, :] = tile[:rows].astype(jnp.bfloat16)
    outs.append(pltpu.make_async_copy(wout, w_hbm, out_sem.at[2]))
    outs[-1].start()
    for copy in sent:
        copy.wait_send()
    for copy in outs:
        copy.wait()


def per_device(activations, out_grad, projector, moment_one, moment_two):
    bf16, f32 = jnp.bfloat16, jnp.float32
    dma = pltpu.SemaphoreType.DMA
    return pl.pallas_call(
        kernel,
        out_shape=(
            jax.ShapeDtypeStruct((COLS, OUT), bf16),
            jax.ShapeDtypeStruct((OWN, COLS), f32),
            jax.ShapeDtypeStruct((OWN, COLS), f32),
        ),
        in_specs=[pl.BlockSpec(memory_space=pl.ANY)] * 5,
        out_specs=[pl.BlockSpec(memory_space=pl.ANY)] * 3,
        scratch_shapes=[
            pltpu.VMEM((ROWS, DM), bf16),
            pltpu.VMEM((DM, RANK), bf16),
            pltpu.VMEM((TOK, COLS), bf16),
            pltpu.VMEM((OUT, RANK), bf16),
            pltpu.VMEM((OWN, COLS), f32),
            pltpu.VMEM((OWN, COLS), f32),
            pltpu.VMEM((OWN, COLS), f32),
            pltpu.VMEM((OWN, COLS), f32),
            pltpu.VMEM((COLS, OUT), bf16),
            pltpu.VMEM((NT, ROWS, RANK), bf16),
            pltpu.VMEM((TOK, RANK), bf16),
            pltpu.VMEM((ND, OWN, WIDE), f32),
            pltpu.VMEM((28, OWN, WIDE), bf16),
            pltpu.VMEM((28, OWN, WIDE), bf16),
            pltpu.VMEM((3, OWN, WIDE), bf16),
            pltpu.VMEM((3, OWN, WIDE), bf16),
            pltpu.VMEM((ND, OWN, WIDE), bf16),
            dma((DM // KC + 5,)),
            dma((3,)),
            dma((23,)),
            dma((NT,)),
            dma((28,)),
            dma((28,)),
            dma((3,)),
            dma((3,)),
            dma((31,)),
            dma((ND,)),
        ],
        compiler_params=pltpu.CompilerParams(
            collective_id=0, has_side_effects=True, vmem_limit_bytes=50 * 2**20
        ),
        name="galore_step",
    )(activations, out_grad, projector, moment_one, moment_two)


def solution(mesh):
    placed = (
        P("dp", "tensor"),
        P(("dp", "tensor"), None),
        P(),
        P("dp", "tensor"),
        P("dp", "tensor"),
    )
    return jax.shard_map(
        per_device,
        mesh=mesh,
        in_specs=placed,
        out_specs=(P("tensor", "dp"), P("dp", "tensor"), P("dp", "tensor")),
        check_vma=False,
    )
```

time: 407 us -> 87.2 us (0.21)
  waiting for transfers between devices: 343 us -> 0 us
  Pallas kernels: 0 us -> 79.6 us
  blocking collectives: 36.4 us -> 0 us
  between operations: 14.1 us -> 0.65 us
  matrix products: 11.1 us -> 0 us
  local copies, waits for them, and re-layouts: 0.02 us -> 6.65 us
    reduce_scatter x1 -> x0, waiting for transfers between devices: 249 us -> none  [per_device(): lax.psum_scatter(lax.dot_general(projected, activations, (((0,), (0,)), (...]
    all_gather x1 -> x0, waiting for transfers between devices: 94.4 us -> none  [per_device(): gathered_update = lax.all_gather(update, 'dp', axis=0, tiled=True)]
    pallas_call x0 -> x1, Pallas kernels: none -> 79.6 us  [per_device(): pl.pallas_call(kernel, out_shape=(jax.ShapeDtypeStruct((COLS, OUT), bf16)...]
    all_gather x1 -> x0, blocking collectives: 36.4 us -> none  [per_device(): projected = lax.all_gather(local_rows, 'tensor', axis=0, tiled=True)]
    dot_general x3 -> x0, matrix products: 11.1 us -> none  [the longest x1 5.26 us: per_device(): jnp.dot(out_grad, projector, preferred_element_type=jnp.float32)]
    unnamed x6 -> x11, local copies, waits for them, and re-layouts: 0.02 us -> 6.65 us
  transfers between devices with their start and end apart: 2 -> 0, of which waited for: 2 -> 0; matrix products, arithmetic and copies ran while one was open for 0% -> 0% of each run, Pallas kernels for 0% -> 0%
where the time goes in v1:
time: 87.2 us; the launch traced here: 86.9 us
  Pallas kernels  79.6 us (91%)
  local copies, waits for them, and re-layouts  6.65 us (8%)
    pallas_call x1, Pallas kernels, per_device(): pl.pallas_call(kernel, out_shape=(jax.ShapeDtypeStruct((COLS, OUT), bf16)...  79.6 us
    unnamed x11, local copies, waits for them, and re-layouts  6.65 us

profile of v1, /device:TPU:2, one launch (start us, length us, event | category | flops | bytes accessed | tf_op | source)
XLA Modules:
  0.0 86.9 jit_solution(10013708764289579921)
XLA Ops:
  0.6 0.0 copy-start
  0.6 1.7 %copy-done = bf16[960,1232]{1,0:T(8,128)(2,1)S(1)} copy-done((bf16[960,1232]{1,0:T(8,128)(2,1)S(1)}, bf16[960,1232]{1,0:T(8,128)(2,1)}, u32[]{:S(2)}) %copy-start) | copy-done | bytes 2365464
  2.3 0.0 copy-start.1
  2.3 1.1 %copy-done.1 = bf16[40,8192]{1,0:T(8,128)(2,1)S(1)} copy-done((bf16[40,8192]{1,0:T(8,128)(2,1)S(1)}, bf16[40,8192]{1,0:T(8,128)(2,1)}, u32[]{:S(2)}) %copy-start.1) | copy-done | bytes 655384
  3.4 0.0 copy-start.2
  3.4 0.9 %copy-done.2 = f32[16,1232]{1,0:T(8,128)S(1)} copy-done((f32[16,1232]{1,0:T(8,128)S(1)}, f32[16,1232]{1,0:T(8,128)}, u32[]{:S(2)}) %copy-start.2) | copy-done | bytes 78872
  4.3 0.0 copy-start.3
  4.3 0.9 %copy-done.3 = f32[16,1232]{1,0:T(8,128)S(1)} copy-done((f32[16,1232]{1,0:T(8,128)S(1)}, f32[16,1232]{1,0:T(8,128)}, u32[]{:S(2)}) %copy-start.3) | copy-done | bytes 78872
  5.2 79.6 %galore_step.1 = (bf16[1232,256]{1,0:T(8,128)(2,1)S(1)}, f32[16,1232]{1,0:T(8,128)S(1)}, f32[16,1232]{1,0:T(8,128)S(1)}) custom-call(bf16[960,1232]{1,0:T(8,128)(2,1)S(1)} %copy-done, bf16[40,8192]{1,0:T(8,128)(2,1)S(1)} %copy-done.1, bf16[8192,512]{1,0:T(8,128)(2,1)} %proj_hbm.1, f32[16,1232]{1,0:T(8,128)S(1)} %copy-done.2, f32[16,1232]{1,0:T(8,128)S(1)} %copy-done.3), custom_call_target="tpu_custom_call" | custom-call | tf_op jit(solution)/shard_map/galore_step/pallas_call | solution.py:299
  84.8 0.8 copy.11
  85.7 0.6 copy.12
  86.3 0.6 copy.13
Async XLA Ops:
  0.6 1.7 %copy-start = (bf16[960,1232]{1,0:T(8,128)(2,1)S(1)}, bf16[960,1232]{1,0:T(8,128)(2,1)}, u32[]{:S(2)}) copy-start(bf16[960,1232]{1,0:T(8,128)(2,1)} %act_hbm.1) | copy-start | bytes 7096324
  2.3 1.1 %copy-start.1 = (bf16[40,8192]{1,0:T(8,128)(2,1)S(1)}, bf16[40,8192]{1,0:T(8,128)(2,1)}, u32[]{:S(2)}) copy-start(bf16[40,8192]{1,0:T(8,128)(2,1)} %og_hbm.1) | copy-start | bytes 1966084
  3.4 0.9 %copy-start.2 = (f32[16,1232]{1,0:T(8,128)S(1)}, f32[16,1232]{1,0:T(8,128)}, u32[]{:S(2)}) copy-start(f32[16,1232]{1,0:T(8,128)} %m1_hbm.1) | copy-start | bytes 236548
  4.3 0.9 %copy-start.3 = (f32[16,1232]{1,0:T(8,128)S(1)}, f32[16,1232]{1,0:T(8,128)}, u32[]{:S(2)}) copy-start(f32[16,1232]{1,0:T(8,128)} %m2_hbm.1) | copy-start | bytes 236548
